TPU v7x, 256 devices: a whole 4x4x8 slice. The times are simulated.
256 devices in a mesh: row: 8 (over x, core), col: 16 (over z, y_hi), layer: 2 (over y_lo).
Axes of the slice: x: 4, y: 4 (y_hi: 2, y_lo: 2; y = y_hi * 2 + y_lo), z: 8, core: 2. Of those that a mesh axis runs over, the one named last changes fastest.
Arguments:
- interface_panel: float32 [2048, 1024], P('col', 'row'), may hold values from -6 to 6
- coupling: float32 [2, 2, 2048, 2048], P('layer', None, 'row', 'col'), may hold values from -0.0625 to 0.0625
- solved_coupling: float32 [8192, 1024], P(('layer', 'col'), 'row'), may hold values from -6 to 6
Outputs:
- schur_panel: float32 [2048, 1024], P('col', 'row')
All inputs are finite; a program needn't handle non-finite values.
Results may differ from a plain program's by a relative error of at most 0.00007.
Values sent between devices are 32-bit elements; how exact they have to be, the bound alone decides.
A program may use at most 64 MiB of HBM per device.

v0:
```python
import jax
import jax.numpy as jnp
from jax import lax
from jax.sharding import PartitionSpec as P


def shards(interface_panel, coupling, solved_coupling):
    blocks = coupling[0]
    depth = blocks.shape[0] * blocks.shape[1] * lax.axis_size("row")
    gathered_b = lax.all_gather(blocks, "row", axis=1, tiled=True).reshape(depth, blocks.shape[2])
    gathered_y = lax.all_gather(solved_coupling, "col", axis=0, tiled=True)
    partial = lax.dot_general(
        gathered_b,
        gathered_y,
        (((0,), (0,)), ((), ())),
        precision=lax.Precision.HIGHEST,
        preferred_element_type=jnp.float32,
    )
    other = lax.ppermute(partial, "layer", [(0, 1), (1, 0)])
    return interface_panel - (partial + other)


def solution(mesh):
    return jax.shard_map(
        shards,
        mesh=mesh,
        in_specs=(P("col", "row"), P("layer", None, "row", "col"), P(("layer", "col"), "row")),
        out_specs=P("col", "row"),
        check_vma=False,
    )
```

profile of v0, /device:TPU:2, one launch (start us, length us, event | category | flops | bytes accessed | tf_op | source)
XLA Modules:
  0.0 145.9 jit_solution(16994233739036828383)
XLA Ops:
  6.5 0.0 all-gather.6.cloned.1.call-start
  6.5 0.7 all-gather.6.cloned.1.call-update
  7.3 0.0 all-gather.4.cloned.1.call-start
  7.3 0.7 all-gather.4.cloned.1.call-update
  8.0 31.0 %all-gather.6.cloned.1.call-done = f32[1,2,2048,128]{3,2,1,0:T(8,128)} async-done(((f32[1,2,256,128]{3,2,1,0:T(8,128)}), f32[1,2,2048,128]{3,2,1,0:T(8,128)}) %all-gather.6.cloned.1.call-update) | async-done | bytes 2097168 | tf_op jit(solution)/shard_map/all_gather | solution.py:10
  39.0 89.4 %all-gather.4.cloned.1.call-done = f32[4096,128]{1,0:T(8,128)} async-done(((f32[256,128]{1,0:T(8,128)}), f32[4096,128]{1,0:T(8,128)}) %all-gather.4.cloned.1.call-update) | async-done | bytes 2097168 | tf_op jit(solution)/shard_map/all_gather | solution.py:11
  128.4 0.0 copy-start
  128.4 5.7 %fusion = f32[128,128]{1,0:T(8,128)S(1)} fusion(f32[4096,128]{1,0:T(8,128)} %bitcast.3, f32[4096,128]{1,0:T(8,128)} %all-gather.4.cloned.1.call-done), kind=kOutput, calls=%fused_computation.1 | convolution fusion | flops 805306368 | bytes 4259840 | tf_op jit(solution)/shard_map/dot_general | solution.py:12
  134.1 0.7 collective-permute-start
  134.7 3.7 %collective-permute-done = f32[128,128]{1,0:T(8,128)S(1)} collective-permute-done((f32[128,128]{1,0:T(8,128)S(1)}, f32[128,128]{1,0:T(8,128)S(1)}, u32[]{:S(2)}, u32[]{:S(2)}) %collective-permute-start) | collective-permute-done | bytes 65568 | tf_op jit(solution)/shard_map/ppermute | solution.py:19
  138.4 0.0 copy-done
  138.4 0.6 add_subtract_fusion
Async XLA Ops:
  6.5 32.4 %all-gather.6.cloned.1.call-start = ((), (), s32[]{:S(2)}) async-start(), calls=%async_computation.1 | async-start | bytes 2359296 | tf_op jit(solution)/shard_map/all_gather | solution.py:10
  7.3 121.1 %all-gather.4.cloned.1.call-start = ((), (), s32[]{:S(2)}) async-start(), calls=%async_computation | async-start | bytes 2228224 | tf_op jit(solution)/shard_map/all_gather | solution.py:11
  128.4 10.1 %copy-start = (f32[128,128]{1,0:T(8,128)S(1)}, f32[128,128]{1,0:T(8,128)}, u32[]{:S(2)}) copy-start(f32[128,128]{1,0:T(8,128)} %param.3) | copy-start | bytes 196612
  134.1 4.4 %collective-permute-start = (f32[128,128]{1,0:T(8,128)S(1)}, f32[128,128]{1,0:T(8,128)S(1)}, u32[]{:S(2)}, u32[]{:S(2)}) collective-permute-start(f32[128,128]{1,0:T(8,128)S(1)} %fusion), channel_id=1, source_target_pairs={{0,1},{1,0},{2,3},{3,2},{4,5},{5,4},{6,7},{7,6},{8,9},{9,8},{10,11... | collective-permute-start | bytes 196616 | tf_op jit(solution)/shard_map/ppermute | solution.py:19
Sparse Core Ops, SparseCore 0:
  9.2 29.7 all-gather.5
  41.6 86.7 all-gather.3
where the time goes:
time: 146 us
  waiting for transfers between devices  125 us (86%)
  between operations  13.4 us (9%)
  matrix products  5.7 us (4%)
    all_gather x1, waiting for transfers between devices, shards(): gathered_y = lax.all_gather(solved_coupling, 'col', axis=0, tiled=True)  89.4 us
    all_gather x1, waiting for transfers between devices, shards(): lax.all_gather(blocks, 'row', axis=1, tiled=True)  31 us
    dot_general x1, matrix products, shards(): lax.dot_general(gathered_b, gathered_y, (((0,), (0,)), ((), ())), precisi...  5.7 us
    ppermute x1, waiting for transfers between devices, shards(): other = lax.ppermute(partial, 'layer', [(0, 1), (1, 0)])  3.68 us
  transfers between devices with their start and end apart: 3, of which 3 were waited for; matrix products, arithmetic and copies ran while one was open for 0% of the time, Pallas kernels for 0%

commit v1 on v0

--- a/solution.py
+++ b/solution.py
@@ -7,7 +7,20 @@
 def shards(interface_panel, coupling, solved_coupling):
     blocks = coupling[0]
     depth = blocks.shape[0] * blocks.shape[1] * lax.axis_size("row")
-    gathered_b = lax.all_gather(blocks, "row", axis=1, tiled=True).reshape(depth, blocks.shape[2])
+
+    def move_spans(xs):
+        axis_n = lax.axis_size("row")
+        vals = [(dev, (dev + 1) % axis_n) for dev in range(axis_n)]
+        sheets = [(dev, (dev - 1) % axis_n) for dev in range(axis_n)]
+        found_now, block_now = ([xs], [xs])
+        for _ in range(axis_n // 2):
+            found_now.append(lax.ppermute(found_now[-1], "row", vals))
+        for _ in range((axis_n - 1) // 2):
+            block_now.append(lax.ppermute(block_now[-1], "row", sheets))
+        arr_now = jnp.concatenate([*found_now[::-1], *block_now[1:]], 1)
+        return jnp.roll(arr_now, (lax.axis_index("row") - axis_n // 2) * xs.shape[1], 1)
+
+    gathered_b = move_spans(blocks).reshape(depth, blocks.shape[2])
     gathered_y = lax.all_gather(solved_coupling, "col", axis=0, tiled=True)
     partial = lax.dot_general(
         gathered_b,

time: 146 us -> 116 us (0.79)
  waiting for transfers between devices: 125 us -> 88.3 us
  starting transfers between devices: 0.71 us -> 6.44 us
    all_gather x1 -> x0, waiting for transfers between devices: 31 us -> none  [shards(): lax.all_gather(blocks, 'row', axis=1, tiled=True)]
    all_gather x1, waiting for transfers between devices: 89.4 us -> 66.3 us  [shards(): gathered_y = lax.all_gather(solved_coupling, 'col', axis=0, tiled=True)]
    ppermute x0 -> x7, waiting for transfers between devices: none -> 17.6 us  [the longest x4 17.1 us: move_spans(): found_now.append(lax.ppermute(found_now[-1], 'row', vals))]
    ppermute x0 -> x7, starting transfers between devices: none -> 5.77 us  [the longest x3 5.75 us: move_spans(): block_now.append(lax.ppermute(block_now[-1], 'row', sheets))]
  transfers between devices with their start and end apart: 3 -> 9, of which waited for: 3 -> 8; matrix products, arithmetic and copies ran while one was open for 0% -> 1% of each run, Pallas kernels for 0% -> 0%
where the time goes in v1:
time: 116 us; the launch traced here: 115 us
  waiting for transfers between devices  88.3 us (76%)
  between operations  13.6 us (12%)
  starting transfers between devices  6.44 us (6%)
  matrix products  5.03 us (4%)
  local copies, waits for them, and re-layouts  1.42 us (1%)
    all_gather x1, waiting for transfers between devices, shards(): gathered_y = lax.all_gather(solved_coupling, 'col', axis=0, tiled=True)  66.3 us
    ppermute x4, waiting for transfers between devices, move_spans(): found_now.append(lax.ppermute(found_now[-1], 'row', vals))  17.1 us
    ppermute x3, starting transfers between devices, move_spans(): block_now.append(lax.ppermute(block_now[-1], 'row', sheets))  5.75 us
    dot_general x1, matrix products, shards(): lax.dot_general(gathered_b, gathered_y, (((0,), (0,)), ((), ())), precisi...  5.03 us
    ppermute x1, waiting for transfers between devices, shards(): other = lax.ppermute(partial, 'layer', [(0, 1), (1, 0)])  3.68 us
  transfers between devices with their start and end apart: 9, of which 8 were waited for; matrix products, arithmetic and copies ran while one was open for 1% of the time, Pallas kernels for 0%

profile of v1, /device:TPU:2, one launch (start us, length us, event | category | flops | bytes accessed | tf_op | source)
XLA Modules:
  0.0 115.4 jit_solution(965974663749398955)
XLA Ops:
  6.5 0.0 copy-start
  6.5 0.0 all-gather.2.cloned.1.call-start
  6.5 0.7 all-gather.2.cloned.1.call-update
  7.3 0.0 collective-permute-start
  7.3 6.0 %collective-permute-done = f32[2,256,128]{2,1,0:T(8,128)S(1)} collective-permute-done((f32[2,256,128]{2,1,0:T(8,128)}, f32[2,256,128]{2,1,0:T(8,128)S(1)}, u32[]{:S(2)}, u32[]{:S(2)}) %collective-permute-start) | collective-permute-done | bytes 262176 | tf_op jit(solution)/shard_map/ppermute | solution.py:17
  13.3 0.0 collective-permute-start.1
  13.3 1.7 %collective-permute-start.4 = (f32[2,256,128]{2,1,0:T(8,128)}, f32[2,256,128]{2,1,0:T(8,128)S(1)}, u32[]{:S(2)}, u32[]{:S(2)}) collective-permute-start(f32[2,256,128]{2,1,0:T(8,128)} %bitcast.8), channel_id=1, source_target_pairs={{0,224},{32,0},{64,32},{96,64},{128,96},{160,128},{192,160},{224,1... | collective-permute-start | bytes 786440 | tf_op jit(solution)/shard_map/ppermute | solution.py:19
  15.0 4.1 %collective-permute-done.1 = f32[2,256,128]{2,1,0:T(8,128)S(1)} collective-permute-done((f32[2,256,128]{2,1,0:T(8,128)S(1)}, f32[2,256,128]{2,1,0:T(8,128)S(1)}, u32[]{:S(2)}, u32[]{:S(2)}) %collective-permute-start.1) | collective-permute-done | bytes 262176 | tf_op jit(solution)/shard_map/ppermute | solution.py:17
  19.1 0.0 collective-permute-start.2
  19.1 0.2 collective-permute-done.4
  19.2 2.1 %collective-permute-start.5 = (f32[2,256,128]{2,1,0:T(8,128)S(1)}, f32[2,256,128]{2,1,0:T(8,128)S(1)}, u32[]{:S(2)}, u32[]{:S(2)}) collective-permute-start(f32[2,256,128]{2,1,0:T(8,128)S(1)} %collective-permute-done.4), channel_id=1, source_target_pairs={{0,224},{32,0},{64,32},{96,64},{128,96},{160,128},{192,160},{224,1... | collective-permute-start | bytes 786440 | tf_op jit(solution)/shard_map/ppermute | solution.py:19
  21.3 3.5 %collective-permute-done.2 = f32[2,256,128]{2,1,0:T(8,128)S(1)} collective-permute-done((f32[2,256,128]{2,1,0:T(8,128)S(1)}, f32[2,256,128]{2,1,0:T(8,128)S(1)}, u32[]{:S(2)}, u32[]{:S(2)}) %collective-permute-start.2) | collective-permute-done | bytes 262176 | tf_op jit(solution)/shard_map/ppermute | solution.py:17
  24.9 0.0 collective-permute-start.3
  24.9 0.3 collective-permute-done.5
  25.2 1.9 %collective-permute-start.6 = (f32[2,256,128]{2,1,0:T(8,128)S(1)}, f32[2,256,128]{2,1,0:T(8,128)S(1)}, u32[]{:S(2)}, u32[]{:S(2)}) collective-permute-start(f32[2,256,128]{2,1,0:T(8,128)S(1)} %collective-permute-done.5), channel_id=1, source_target_pairs={{0,224},{32,0},{64,32},{96,64},{128,96},{160,128},{192,160},{224,1... | collective-permute-start | bytes 786440 | tf_op jit(solution)/shard_map/ppermute | solution.py:19
  27.1 3.5 %collective-permute-done.3 = f32[2,256,128]{2,1,0:T(8,128)S(1)} collective-permute-done((f32[2,256,128]{2,1,0:T(8,128)S(1)}, f32[2,256,128]{2,1,0:T(8,128)S(1)}, u32[]{:S(2)}, u32[]{:S(2)}) %collective-permute-start.3) | collective-permute-done | bytes 262176 | tf_op jit(solution)/shard_map/ppermute | solution.py:17
  30.8 1.0 constant_dynamic-update-slice_fusion.11
  31.8 0.0 collective-permute-done.6
  32.0 0.0 copy-done
  32.1 0.0 copy-start.1
  32.1 0.1 constant_dynamic-slice_fusion
  32.2 66.3 %all-gather.2.cloned.1.call-done = f32[4096,128]{1,0:T(8,128)} async-done(((f32[256,128]{1,0:T(8,128)}), f32[4096,128]{1,0:T(8,128)}) %all-gather.2.cloned.1.call-update) | async-done | bytes 2097168 | tf_op jit(solution)/shard_map/all_gather | solution.py:24
  98.5 5.0 %fusion = f32[128,128]{1,0:T(8,128)S(1)} fusion(f32[4096,128]{1,0:T(8,128)S(1)} %bitcast.6, f32[4096,128]{1,0:T(8,128)} %all-gather.2.cloned.1.call-done), kind=kOutput, calls=%fused_computation.18 | convolution fusion | flops 805306368 | bytes 4259840 | tf_op jit(solution)/shard_map/dot_general | solution.py:25
  103.6 0.7 collective-permute-start.7
  104.2 3.7 %collective-permute-done.7 = f32[128,128]{1,0:T(8,128)S(1)} collective-permute-done((f32[128,128]{1,0:T(8,128)S(1)}, f32[128,128]{1,0:T(8,128)S(1)}, u32[]{:S(2)}, u32[]{:S(2)}) %collective-permute-start.7) | collective-permute-done | bytes 65568 | tf_op jit(solution)/shard_map/ppermute | solution.py:32
  107.9 0.0 copy-done.1
  107.9 0.6 add_subtract_fusion
  (15 shorter events, 0.3 us)
Async XLA Ops:
  6.5 25.4 %copy-start = (f32[1,2,256,128]{3,2,1,0:T(8,128)S(1)}, f32[1,2,256,128]{3,2,1,0:T(8,128)}, u32[]{:S(2)}) copy-start(f32[1,2,256,128]{3,2,1,0:T(8,128)} %param.4) | copy-start | bytes 786436
  6.5 92.0 %all-gather.2.cloned.1.call-start = ((), (), s32[]{:S(2)}) async-start(), calls=%async_computation | async-start | bytes 2228224 | tf_op jit(solution)/shard_map/all_gather | solution.py:24
  7.3 6.0 %collective-permute-start = (f32[2,256,128]{2,1,0:T(8,128)}, f32[2,256,128]{2,1,0:T(8,128)S(1)}, u32[]{:S(2)}, u32[]{:S(2)}) collective-permute-start(f32[2,256,128]{2,1,0:T(8,128)} %bitcast.7), channel_id=1, source_target_pairs={{0,32},{32,64},{64,96},{96,128},{128,160},{160,192},{192,224},{224... | collective-permute-start | bytes 786440 | tf_op jit(solution)/shard_map/ppermute | solution.py:17
  13.3 5.8 %collective-permute-start.1 = (f32[2,256,128]{2,1,0:T(8,128)S(1)}, f32[2,256,128]{2,1,0:T(8,128)S(1)}, u32[]{:S(2)}, u32[]{:S(2)}) collective-permute-start(f32[2,256,128]{2,1,0:T(8,128)S(1)} %collective-permute-done), channel_id=1, source_target_pairs={{0,32},{32,64},{64,96},{96,128},{128,160},{160,192},{192,224},{224... | collective-permute-start | bytes 786440 | tf_op jit(solution)/shard_map/ppermute | solution.py:17
  13.3 6.0 %collective-permute-start.4 = (f32[2,256,128]{2,1,0:T(8,128)}, f32[2,256,128]{2,1,0:T(8,128)S(1)}, u32[]{:S(2)}, u32[]{:S(2)}) collective-permute-start(f32[2,256,128]{2,1,0:T(8,128)} %bitcast.8), channel_id=1, source_target_pairs={{0,224},{32,0},{64,32},{96,64},{128,96},{160,128},{192,160},{224,1... | collective-permute-start | bytes 786440 | tf_op jit(solution)/shard_map/ppermute | solution.py:19
  19.1 5.8 %collective-permute-start.2 = (f32[2,256,128]{2,1,0:T(8,128)S(1)}, f32[2,256,128]{2,1,0:T(8,128)S(1)}, u32[]{:S(2)}, u32[]{:S(2)}) collective-permute-start(f32[2,256,128]{2,1,0:T(8,128)S(1)} %collective-permute-done.1), channel_id=1, source_target_pairs={{0,32},{32,64},{64,96},{96,128},{128,160},{160,192},{192,224},{224... | collective-permute-start | bytes 786440 | tf_op jit(solution)/shard_map/ppermute | solution.py:17
  19.2 6.0 %collective-permute-start.5 = (f32[2,256,128]{2,1,0:T(8,128)S(1)}, f32[2,256,128]{2,1,0:T(8,128)S(1)}, u32[]{:S(2)}, u32[]{:S(2)}) collective-permute-start(f32[2,256,128]{2,1,0:T(8,128)S(1)} %collective-permute-done.4), channel_id=1, source_target_pairs={{0,224},{32,0},{64,32},{96,64},{128,96},{160,128},{192,160},{224,1... | collective-permute-start | bytes 786440 | tf_op jit(solution)/shard_map/ppermute | solution.py:19
  24.9 5.8 %collective-permute-start.3 = (f32[2,256,128]{2,1,0:T(8,128)S(1)}, f32[2,256,128]{2,1,0:T(8,128)S(1)}, u32[]{:S(2)}, u32[]{:S(2)}) collective-permute-start(f32[2,256,128]{2,1,0:T(8,128)S(1)} %collective-permute-done.2), channel_id=1, source_target_pairs={{0,32},{32,64},{64,96},{96,128},{128,160},{160,192},{192,224},{224... | collective-permute-start | bytes 786440 | tf_op jit(solution)/shard_map/ppermute | solution.py:17
  25.2 6.6 %collective-permute-start.6 = (f32[2,256,128]{2,1,0:T(8,128)S(1)}, f32[2,256,128]{2,1,0:T(8,128)S(1)}, u32[]{:S(2)}, u32[]{:S(2)}) collective-permute-start(f32[2,256,128]{2,1,0:T(8,128)S(1)} %collective-permute-done.5), channel_id=1, source_target_pairs={{0,224},{32,0},{64,32},{96,64},{128,96},{160,128},{192,160},{224,1... | collective-permute-start | bytes 786440 | tf_op jit(solution)/shard_map/ppermute | solution.py:19
  32.1 75.9 %copy-start.1 = (f32[128,128]{1,0:T(8,128)S(1)}, f32[128,128]{1,0:T(8,128)}, u32[]{:S(2)}) copy-start(f32[128,128]{1,0:T(8,128)} %param.3) | copy-start | bytes 196612
  103.6 4.4 %collective-permute-start.7 = (f32[128,128]{1,0:T(8,128)S(1)}, f32[128,128]{1,0:T(8,128)S(1)}, u32[]{:S(2)}, u32[]{:S(2)}) collective-permute-start(f32[128,128]{1,0:T(8,128)S(1)} %fusion), channel_id=1, source_target_pairs={{0,1},{1,0},{2,3},{3,2},{4,5},{5,4},{6,7},{7,6},{8,9},{9,8},{10,11... | collective-permute-start | bytes 196616 | tf_op jit(solution)/shard_map/ppermute | solution.py:32
Sparse Core Ops, SparseCore 0:
  9.9 88.5 all-gather.1
